TPU v7x, 128 devices: a whole 4x4x4 slice. The times are simulated.
128 devices in a mesh: segment: 8 (over x, core), patch: 16 (over y, z).
Axes of the slice: x: 4, y: 4, z: 4, core: 2. Of those that a mesh axis runs over, the one named last changes fastest.
Arguments:
- latent: bfloat16 [2, 64, 64, 640], P(None, 'patch'), may hold values from -6 to 6
- stale_attn: bfloat16 [8, 2, 64, 64, 640], P('segment', None, 'patch'), may hold values from -6 to 6
- stale_edge: bfloat16 [8, 2, 32, 64, 640], P('segment', None, 'patch'), may hold values from -6 to 6
- norm_attn: float32 [8, 640], P('segment'), may hold values from 0.1 to 1.9
- query_w: bfloat16 [8, 640, 640], P('segment'), may hold values from -0.5 to 0.5
- key_w: bfloat16 [8, 640, 640], P('segment'), may hold values from -0.25 to 0.25
- value_w: bfloat16 [8, 640, 640], P('segment'), may hold values from -0.25 to 0.25
- out_w: bfloat16 [8, 640, 640], P('segment'), may hold values from -0.75 to 0.75
- norm_conv: float32 [8, 640], P('segment'), may hold values from 0.1 to 1.9
- conv_w: bfloat16 [8, 3, 3, 640, 640], P('segment'), may hold values from -0.078125 to 0.078125
Outputs:
- denoised: float32 [2, 64, 64, 640], P(None, 'patch', 'segment')
All inputs are finite; a program needn't handle non-finite values.
Results may differ from a plain program's by a relative error of at most 0.035.
Values may be sent and summed in bfloat16 or wider, within the bound.
No kernel may reach another device: no remote copies, remote signals or barrier semaphores. Data moves between devices by JAX's collectives and lax.ppermute only.
A program may use at most 128 MiB of HBM per device.

v0:
```python
import jax
import jax.numpy as jnp
from jax import lax
from jax.sharding import PartitionSpec as P

HEADS = 10


def padded(cells, sides, width):
    for axis, dim in sides:
        count = lax.axis_size(axis)
        ends = count - 1
        head = lax.slice_in_dim(cells, 0, width, axis=dim)
        tail = lax.slice_in_dim(cells, cells.shape[dim] - width, cells.shape[dim], axis=dim)
        cells = jnp.concatenate(
            [
                lax.ppermute(tail, axis, [(i, (i + 1) % count) for i in range(ends)]),
                cells,
                lax.ppermute(head, axis, [((i + 1) % count, i) for i in range(ends)]),
            ],
            axis=dim,
        )
    return cells


def passed_along(value, axis, by):
    length = lax.axis_size(axis)
    pairs = [(i, i + by) for i in range(length) if 0 <= i + by < length]
    return lax.ppermute(value, axis, pairs)


def layer_norm(values, gain_vec):
    floats = values.astype(jnp.float32)
    center = floats - jnp.mean(floats, axis=-1, keepdims=True)
    spread = jnp.mean(center * center, axis=-1, keepdims=True)
    return center * lax.rsqrt(spread + 1e-05) * gain_vec


def project(row_data, weight):
    flattened = row_data.reshape(-1, row_data.shape[-1])
    result = jnp.dot(flattened, weight, preferred_element_type=jnp.float32).astype(jnp.bfloat16)
    return result.reshape(row_data.shape[:-1] + (weight.shape[1],))


def shards(
    latent, stale_attn, stale_edge, norm_attn, query_w, key_w, value_w, out_w, norm_conv, conv_w
):
    segment_index = lax.axis_index("segment")
    segment_count = lax.axis_size("segment")
    patch_index = lax.axis_index("patch")
    micro_count, row_count, col_count, channels = latent.shape
    head_count = HEADS
    head_dim = channels // head_count
    cell_count = row_count * col_count
    score_scale = head_dim ** (-0.5)
    gain_attn = norm_attn[0]
    gain_conv = norm_conv[0]
    query_weight = query_w[0]
    key_weight = key_w[0]
    value_weight = value_w[0]
    out_weight = out_w[0]
    kernel = conv_w[0]
    stale_normed = layer_norm(stale_attn[0], gain_attn).astype(jnp.bfloat16)
    near_keys = project(stale_normed, key_weight)
    near_values = project(stale_normed, value_weight)
    far_keys, far_values = (
        lax.all_gather(near_keys, "patch", axis=1, tiled=True),
        lax.all_gather(near_values, "patch", axis=1, tiled=True),
    )
    far_keys = far_keys.reshape(micro_count, -1, channels)
    far_values = far_values.reshape(micro_count, -1, channels)
    key_block = 4 * cell_count
    block_total = far_keys.shape[1] // key_block
    edge_rows = padded(stale_edge[0], (("patch", 1),), 1)

    def attend(queries, fresh_key, fresh_value, micro_pos):
        query_heads = queries.reshape(cell_count, head_count, head_dim)
        keys_now = lax.dynamic_index_in_dim(far_keys, micro_pos, 0, keepdims=False)
        values_now = lax.dynamic_index_in_dim(far_values, micro_pos, 0, keepdims=False)
        own_keys = fresh_key.reshape(cell_count, head_count, head_dim)
        own_values = fresh_value.reshape(cell_count, head_count, head_dim)
        own_scores = (
            jnp.einsum("qhd,khd->hqk", query_heads, own_keys, preferred_element_type=jnp.float32)
            * score_scale
        )
        own_exp = jnp.exp(own_scores)
        totals = jnp.sum(own_exp, axis=-1)
        context_sum = jnp.einsum(
            "hqk,khd->qhd",
            own_exp.astype(jnp.bfloat16),
            own_values,
            preferred_element_type=jnp.float32,
        )

        def add_block(block_no, carry):
            sums, partial_value = carry
            key_part = lax.dynamic_slice_in_dim(
                keys_now, block_no * key_block, key_block, 0
            ).reshape(key_block, head_count, head_dim)
            value_part = lax.dynamic_slice_in_dim(
                values_now, block_no * key_block, key_block, 0
            ).reshape(key_block, head_count, head_dim)
            scores = (
                jnp.einsum(
                    "qhd,khd->hqk", query_heads, key_part, preferred_element_type=jnp.float32
                )
                * score_scale
            )
            owner_patch = (
                block_no * key_block + jnp.arange(key_block, dtype=jnp.int32)
            ) // cell_count
            kept_mask = (owner_patch != patch_index).astype(jnp.float32)
            exp_scores = jnp.exp(scores) * kept_mask
            sums = sums + jnp.sum(exp_scores, axis=-1)
            partial_value = partial_value + jnp.einsum(
                "hqk,khd->qhd",
                exp_scores.astype(jnp.bfloat16),
                value_part,
                preferred_element_type=jnp.float32,
            )
            return (sums, partial_value)

        totals, context_sum = lax.fori_loop(0, block_total, add_block, (totals, context_sum))
        context = context_sum / jnp.transpose(totals)[:, :, None]
        return context.reshape(cell_count, channels).astype(jnp.bfloat16)

    def apply_block(current, micro_pos):
        normed = layer_norm(current, gain_attn).astype(jnp.bfloat16)
        queries = project(normed, query_weight)
        fresh_key = project(normed, key_weight)
        fresh_value = project(normed, value_weight)
        context = attend(queries, fresh_key, fresh_value, micro_pos)
        attn_out = jnp.dot(context, out_weight, preferred_element_type=jnp.float32)
        x_mid = current + attn_out.reshape(row_count, col_count, channels)
        conv_in = jax.nn.silu(layer_norm(x_mid, gain_conv)).astype(jnp.bfloat16)
        edges_now = lax.dynamic_index_in_dim(edge_rows, micro_pos, 0, keepdims=False)
        extended = jnp.concatenate([edges_now[0:1], conv_in, edges_now[3:4]], 0)
        extended = jnp.pad(extended, ((0, 0), (1, 1), (0, 0)))
        conv_sum = jnp.zeros((cell_count, channels), jnp.float32)
        for row_tap in range(3):
            for col_tap in range(3):
                shifted = extended[
                    row_tap : row_tap + row_count, col_tap : col_tap + col_count
                ].reshape(-1, channels)
                conv_sum = conv_sum + jnp.dot(
                    shifted, kernel[row_tap, col_tap], preferred_element_type=jnp.float32
                )
        return x_mid + conv_sum.reshape(row_count, col_count, channels)

    def advance(tick_index, carry):
        incoming, results = carry
        micro = tick_index - segment_index
        active = (micro >= 0) & (micro < micro_count)
        micro_pos = jnp.clip(micro, 0, micro_count - 1)
        first_input = lax.dynamic_index_in_dim(latent, micro_pos, 0, keepdims=False).astype(
            jnp.float32
        )
        block_input = jnp.where(segment_index == 0, first_input, incoming)
        produced = lax.cond(
            active, lambda: apply_block(block_input, micro_pos), lambda: jnp.zeros_like(incoming)
        )
        is_last = active & (segment_index == segment_count - 1)
        results = jnp.where(
            is_last, lax.dynamic_update_index_in_dim(results, produced, micro_pos, 0), results
        )
        incoming = passed_along(produced.astype(jnp.bfloat16), "segment", 1).astype(produced.dtype)
        return (incoming, results)

    start_input = jnp.zeros((row_count, col_count, channels), jnp.float32)
    start_results = jnp.zeros((micro_count, row_count, col_count, channels), jnp.float32)
    final_in, results = lax.fori_loop(
        0, micro_count + segment_count - 1, advance, (start_input, start_results)
    )
    return lax.psum_scatter(
        results.astype(jnp.bfloat16), "segment", scatter_dimension=2, tiled=True
    ).astype(jnp.float32)


def solution(mesh):
    in_specs = (
        P(None, "patch", None, None),
        P("segment", None, "patch", None, None),
        P("segment", None, "patch", None, None),
        P("segment", None),
        P("segment", None, None),
        P("segment", None, None),
        P("segment", None, None),
        P("segment", None, None),
        P("segment", None),
        P("segment", None, None, None, None),
    )
    out_specs = P(None, "patch", "segment", None)
    return jax.shard_map(shards, mesh=mesh, in_specs=in_specs, out_specs=out_specs, check_vma=False)
```

profile of v0, /device:TPU:0, one launch (start us, length us, event | category | flops | bytes accessed | tf_op | source)
XLA Modules:
  0.0 809.1 jit_solution(14509728789227207962)
XLA Ops:
  17.0 3.9 collective-permute-start.1
  24.4 4.3 collective-permute-done.2
  29.6 67.6 %all-gather.3.cloned.1.call-done = bf16[2,64,64,640]{3,2,1,0:T(8,128)(2,1)} async-done(((bf16[2,4,64,640]{3,2,1,0:T(8,128)(2,1)}), bf16[2,64,64,640]{3,2,1,0:T(8,128)(2,1)}) %all-gather.3.cloned.1.call-update) | async-done | bytes 10485776 | tf_op jit(solution)/shard_map/all_gather | solution.py:67
  97.2 14.8 %copy.34 = bf16[2,4096,640]{1,2,0:T(8,128)(2,1)} copy(bf16[2,4096,640]{2,1,0:T(8,128)(2,1)} %bitcast.213) | data formatting | bytes 20971520
  112.1 67.4 %all-gather.5.cloned.1.call-done = bf16[2,64,64,640]{3,2,1,0:T(8,128)(2,1)} async-done(((bf16[2,4,64,640]{3,2,1,0:T(8,128)(2,1)}), bf16[2,64,64,640]{3,2,1,0:T(8,128)(2,1)}) %all-gather.5.cloned.1.call-update) | async-done | bytes 10485776 | tf_op jit(solution)/shard_map/all_gather | solution.py:68
  179.5 14.9 %copy.35 = bf16[2,4096,640]{1,2,0:T(8,128)(2,1)} copy(bf16[2,4096,640]{2,1,0:T(8,128)(2,1)} %bitcast.214) | data formatting | bytes 20971520
  195.4 401.9 %while.41 = (s32[]{:T(128)}, f32[4,64,640]{2,1,0:T(8,128)S(1)}, bf16[2,4,64,640]{3,2,1,0:T(8,128)(2,1)}, s32[]{:T(128)}, pred[]{:T(512)}, /*index=5*/bf16[2,4,64...) while((s32[]{:T(128)}, f32[4,64,640]{2,1,0:T(8,128)S(1)}, ...), condition=%wide.region_13.14_spmd.clone, body=%wide.region_2.13_spmd.clone.sunk | while | flops 3595085824 | bytes 135619984 | solution.py:171
  195.6 58.3 %conditional.3 = (bf16[4,64,640]{2,1,0:T(8,128)(2,1)S(1)}) conditional(s32[]{:T(128)} %convert_element_type.192, () %tuple.104, (pred[]{:T(512)}, bf16[2,4,64,640]{3,2,1,0:T(8,128)(2,1)S(1)}, s32[]{:T(128)}, s32[]{:T(128)}, f32[1,640]{1,0:T(1,128)S(1)}, /*index=5*/bf16[640,640]{1,0:T(8,128)(2,1)}, bf16[640,640]{1,0:T(8,128)(2,1)}, ...), branch_computations={%region_3.3_spmd, %region_4.12_spmd.clone} | conditional | flops 3594758144 | bytes 132342232 | solution.py:159
  204.8 9.7 %dynamic-slice_bitcast_fusion = (bf16[4096,640]{0,1:T(8,128)(2,1)}, bf16[4096,640]{0,1:T(8,128)(2,1)}) fusion(bf16[2,4096,640]{1,2,0:T(8,128)(2,1)} %get-tuple-element.763, s32[]{:T(128)S(6)} %select_n.87, bf16[2,4096,640]{1,2,0:T(8,128)(2,1)} %get-tuple-element.761), kind=kLoop, calls=%fused_computation.22 | loop fusion | bytes 20971524 | tf_op jit(solution)/shard_map/while/body/eval_jaxpr/cond/branch_1_fun/jit(dynamic_index_in_dim)/squeeze | solution.py:79
  214.5 27.1 %while.40 = (s32[]{:T(128)}, f32[10,256]{1,0:T(8,128)S(1)}, f32[256,10,64]{0,2,1:T(8,128)S(1)}, bf16[4096,640]{0,1:T(8,128)(2,1)}, bf16[256,10,64]{0,2,1:T(8,128...) while((s32[]{:T(128)}, f32[10,256]{1,0:T(8,128)S(1)}, ...), condition=%wide.region_10.9_spmd, body=%wide.region_8.8_spmd.sunk | while | flops 686999552 | bytes 30527656 | solution.py:123
  216.6 2.8 bitcast_reduce_fusion.2
  223.3 2.8 bitcast_reduce_fusion.2
  230.1 2.8 bitcast_reduce_fusion.2
  257.1 58.3 %conditional.3 = (bf16[4,64,640]{2,1,0:T(8,128)(2,1)S(1)}) conditional(s32[]{:T(128)} %convert_element_type.192, () %tuple.104, (pred[]{:T(512)}, bf16[2,4,64,640]{3,2,1,0:T(8,128)(2,1)S(1)}, s32[]{:T(128)}, s32[]{:T(128)}, f32[1,640]{1,0:T(1,128)S(1)}, /*index=5*/bf16[640,640]{1,0:T(8,128)(2,1)}, bf16[640,640]{1,0:T(8,128)(2,1)}, ...), branch_computations={%region_3.3_spmd, %region_4.12_spmd.clone} | conditional | flops 3594758144 | bytes 132342232 | solution.py:159
  266.4 9.7 %dynamic-slice_bitcast_fusion = (bf16[4096,640]{0,1:T(8,128)(2,1)}, bf16[4096,640]{0,1:T(8,128)(2,1)}) fusion(bf16[2,4096,640]{1,2,0:T(8,128)(2,1)} %get-tuple-element.763, s32[]{:T(128)S(6)} %select_n.87, bf16[2,4096,640]{1,2,0:T(8,128)(2,1)} %get-tuple-element.761), kind=kLoop, calls=%fused_computation.22 | loop fusion | bytes 20971524 | tf_op jit(solution)/shard_map/while/body/eval_jaxpr/cond/branch_1_fun/jit(dynamic_index_in_dim)/squeeze | solution.py:79
  276.0 27.1 %while.40 = (s32[]{:T(128)}, f32[10,256]{1,0:T(8,128)S(1)}, f32[256,10,64]{0,2,1:T(8,128)S(1)}, bf16[4096,640]{0,1:T(8,128)(2,1)}, bf16[256,10,64]{0,2,1:T(8,128...) while((s32[]{:T(128)}, f32[10,256]{1,0:T(8,128)S(1)}, ...), condition=%wide.region_10.9_spmd, body=%wide.region_8.8_spmd.sunk | while | flops 686999552 | bytes 30527656 | solution.py:123
  319.0 62.4 %collective-permute-start = (bf16[4,64,640]{2,1,0:T(8,128)(2,1)S(1)}, bf16[4,64,640]{2,1,0:T(8,128)(2,1)S(1)}, u32[]{:S(2)}, u32[]{:S(2)}) collective-permute-start(bf16[4,64,640]{2,1,0:T(8,128)(2,1)S(1)} %get-tuple-element.1118), channel_id=1, source_target_pairs={{0,16},{16,32},{32,48},{48,64},{64,80},{80,96},{96,112},{1,17},{17... | collective-permute-start | bytes 983048 | tf_op jit(solution)/shard_map/while/body/eval_jaxpr/ppermute | solution.py:29
  383.4 6.6 collective-permute-start
  391.9 64.8 %collective-permute-start = (bf16[4,64,640]{2,1,0:T(8,128)(2,1)S(1)}, bf16[4,64,640]{2,1,0:T(8,128)(2,1)S(1)}, u32[]{:S(2)}, u32[]{:S(2)}) collective-permute-start(bf16[4,64,640]{2,1,0:T(8,128)(2,1)S(1)} %get-tuple-element.1118), channel_id=1, source_target_pairs={{0,16},{16,32},{32,48},{48,64},{64,80},{80,96},{96,112},{1,17},{17... | collective-permute-start | bytes 983048 | tf_op jit(solution)/shard_map/while/body/eval_jaxpr/ppermute | solution.py:29
  458.7 6.6 collective-permute-start
  467.2 55.3 %collective-permute-start = (bf16[4,64,640]{2,1,0:T(8,128)(2,1)S(1)}, bf16[4,64,640]{2,1,0:T(8,128)(2,1)S(1)}, u32[]{:S(2)}, u32[]{:S(2)}) collective-permute-start(bf16[4,64,640]{2,1,0:T(8,128)(2,1)S(1)} %get-tuple-element.1118), channel_id=1, source_target_pairs={{0,16},{16,32},{32,48},{48,64},{64,80},{80,96},{96,112},{1,17},{17... | collective-permute-start | bytes 983048 | tf_op jit(solution)/shard_map/while/body/eval_jaxpr/ppermute | solution.py:29
  524.5 6.6 collective-permute-start
  533.0 62.4 %collective-permute-start = (bf16[4,64,640]{2,1,0:T(8,128)(2,1)S(1)}, bf16[4,64,640]{2,1,0:T(8,128)(2,1)S(1)}, u32[]{:S(2)}, u32[]{:S(2)}) collective-permute-start(bf16[4,64,640]{2,1,0:T(8,128)(2,1)S(1)} %get-tuple-element.1118), channel_id=1, source_target_pairs={{0,16},{16,32},{32,48},{48,64},{64,80},{80,96},{96,112},{1,17},{17... | collective-permute-start | bytes 983048 | tf_op jit(solution)/shard_map/while/body/eval_jaxpr/ppermute | solution.py:29
  600.2 200.8 %reduce-scatter.4.cloned.1.call-done = bf16[8,5120]{1,0:T(8,128)(2,1)} async-done(((bf16[64,5120]{1,0:T(8,128)(2,1)}), bf16[8,5120]{1,0:T(8,128)(2,1)}) %reduce-scatter.4.cloned.1.call-update) | async-done | bytes 81936
  (202 shorter events, 128.2 us)
Async XLA Ops:
  6.5 10.4 %copy-start.3 = (bf16[1,2,2,64,640]{4,3,2,1,0:T(8,128)(2,1)S(1)}, bf16[1,2,2,64,640]{4,3,2,1,0:T(8,128)(2,1)}, u32[]{:S(2)}) copy-start(bf16[1,2,2,64,640]{4,3,2,1,0:T(8,128)(2,1)} %param.18) | copy-start | bytes 983044
  6.5 90.7 %all-gather.3.cloned.1.call-start = ((), (), s32[]{:S(2)}) async-start(), calls=%async_computation.1 | async-start | bytes 11141120 | tf_op jit(solution)/shard_map/all_gather | solution.py:67
  14.1 165.4 %all-gather.5.cloned.1.call-start = ((), (), s32[]{:S(2)}) async-start(), calls=%async_computation.2 | async-start | bytes 11141120 | tf_op jit(solution)/shard_map/all_gather | solution.py:68
  16.9 784.0 %reduce-scatter.4.cloned.1.call-start = ((), (), s32[]{:S(2)}) async-start(), calls=%async_computation.3 | async-start | bytes 737280
  17.0 7.4 collective-permute-start.1
  20.9 7.7 collective-permute-start.2
  179.5 15.8 %copy-start = (bf16[2,4,64,640]{3,2,1,0:T(8,128)(2,1)S(1)}, bf16[2,4,64,640]{3,2,1,0:T(8,128)(2,1)}, u32[]{:S(2)}) copy-start(bf16[2,4,64,640]{3,2,1,0:T(8,128)(2,1)} %param.16) | copy-start | bytes 1966084
  179.5 15.8 %copy-start.4 = (f32[1,640]{1,0:T(1,128)S(1)}, f32[1,640]{1,0:T(1,128)}, u32[]{:S(2)}) copy-start(f32[1,640]{1,0:T(1,128)} %param.19) | copy-start | bytes 7684
  179.5 15.8 %copy-start.5 = (f32[1,640]{1,0:T(1,128)S(1)}, f32[1,640]{1,0:T(1,128)}, u32[]{:S(2)}) copy-start(f32[1,640]{1,0:T(1,128)} %param.24) | copy-start | bytes 7684
  214.5 27.5 %copy-start.1 = (bf16[640,640]{1,0:T(8,128)(2,1)S(1)}, bf16[640,640]{1,0:T(8,128)(2,1)}, u32[]{:S(2)}) copy-start(bf16[640,640]{1,0:T(8,128)(2,1)} %get-tuple-element.766) | copy-start | bytes 2457604 | tf_op jit(solution)/shard_map/while/body/eval_jaxpr/cond
  244.1 7.3 slice-start
  246.4 5.1 slice-start.1
  253.9 3.1 collective-permute-start
  276.0 27.5 %copy-start.1 = (bf16[640,640]{1,0:T(8,128)(2,1)S(1)}, bf16[640,640]{1,0:T(8,128)(2,1)}, u32[]{:S(2)}) copy-start(bf16[640,640]{1,0:T(8,128)(2,1)} %get-tuple-element.766) | copy-start | bytes 2457604 | tf_op jit(solution)/shard_map/while/body/eval_jaxpr/cond
  305.6 7.3 slice-start
  307.9 5.1 slice-start.1
  315.4 3.5 collective-permute-start
  319.0 64.2 %collective-permute-start = (bf16[4,64,640]{2,1,0:T(8,128)(2,1)S(1)}, bf16[4,64,640]{2,1,0:T(8,128)(2,1)S(1)}, u32[]{:S(2)}, u32[]{:S(2)}) collective-permute-start(bf16[4,64,640]{2,1,0:T(8,128)(2,1)S(1)} %get-tuple-element.1118), channel_id=1, source_target_pairs={{0,16},{16,32},{32,48},{48,64},{64,80},{80,96},{96,112},{1,17},{17... | collective-permute-start | bytes 983048 | tf_op jit(solution)/shard_map/while/body/eval_jaxpr/ppermute | solution.py:29
  383.4 8.4 %collective-permute-start = (bf16[4,64,640]{2,1,0:T(8,128)(2,1)S(1)}, bf16[4,64,640]{2,1,0:T(8,128)(2,1)S(1)}, u32[]{:S(2)}, u32[]{:S(2)}) collective-permute-start(bf16[4,64,640]{2,1,0:T(8,128)(2,1)S(1)} %get-tuple-element.1118), channel_id=1, source_target_pairs={{0,16},{16,32},{32,48},{48,64},{64,80},{80,96},{96,112},{1,17},{17... | collective-permute-start | bytes 983048 | tf_op jit(solution)/shard_map/while/body/eval_jaxpr/ppermute | solution.py:29
  391.9 66.7 %collective-permute-start = (bf16[4,64,640]{2,1,0:T(8,128)(2,1)S(1)}, bf16[4,64,640]{2,1,0:T(8,128)(2,1)S(1)}, u32[]{:S(2)}, u32[]{:S(2)}) collective-permute-start(bf16[4,64,640]{2,1,0:T(8,128)(2,1)S(1)} %get-tuple-element.1118), channel_id=1, source_target_pairs={{0,16},{16,32},{32,48},{48,64},{64,80},{80,96},{96,112},{1,17},{17... | collective-permute-start | bytes 983048 | tf_op jit(solution)/shard_map/while/body/eval_jaxpr/ppermute | solution.py:29
  458.7 8.4 %collective-permute-start = (bf16[4,64,640]{2,1,0:T(8,128)(2,1)S(1)}, bf16[4,64,640]{2,1,0:T(8,128)(2,1)S(1)}, u32[]{:S(2)}, u32[]{:S(2)}) collective-permute-start(bf16[4,64,640]{2,1,0:T(8,128)(2,1)S(1)} %get-tuple-element.1118), channel_id=1, source_target_pairs={{0,16},{16,32},{32,48},{48,64},{64,80},{80,96},{96,112},{1,17},{17... | collective-permute-start | bytes 983048 | tf_op jit(solution)/shard_map/while/body/eval_jaxpr/ppermute | solution.py:29
  467.2 57.1 %collective-permute-start = (bf16[4,64,640]{2,1,0:T(8,128)(2,1)S(1)}, bf16[4,64,640]{2,1,0:T(8,128)(2,1)S(1)}, u32[]{:S(2)}, u32[]{:S(2)}) collective-permute-start(bf16[4,64,640]{2,1,0:T(8,128)(2,1)S(1)} %get-tuple-element.1118), channel_id=1, source_target_pairs={{0,16},{16,32},{32,48},{48,64},{64,80},{80,96},{96,112},{1,17},{17... | collective-permute-start | bytes 983048 | tf_op jit(solution)/shard_map/while/body/eval_jaxpr/ppermute | solution.py:29
  524.5 8.4 %collective-permute-start = (bf16[4,64,640]{2,1,0:T(8,128)(2,1)S(1)}, bf16[4,64,640]{2,1,0:T(8,128)(2,1)S(1)}, u32[]{:S(2)}, u32[]{:S(2)}) collective-permute-start(bf16[4,64,640]{2,1,0:T(8,128)(2,1)S(1)} %get-tuple-element.1118), channel_id=1, source_target_pairs={{0,16},{16,32},{32,48},{48,64},{64,80},{80,96},{96,112},{1,17},{17... | collective-permute-start | bytes 983048 | tf_op jit(solution)/shard_map/while/body/eval_jaxpr/ppermute | solution.py:29
  533.0 64.2 %collective-permute-start = (bf16[4,64,640]{2,1,0:T(8,128)(2,1)S(1)}, bf16[4,64,640]{2,1,0:T(8,128)(2,1)S(1)}, u32[]{:S(2)}, u32[]{:S(2)}) collective-permute-start(bf16[4,64,640]{2,1,0:T(8,128)(2,1)S(1)} %get-tuple-element.1118), channel_id=1, source_target_pairs={{0,16},{16,32},{32,48},{48,64},{64,80},{80,96},{96,112},{1,17},{17... | collective-permute-start | bytes 983048 | tf_op jit(solution)/shard_map/while/body/eval_jaxpr/ppermute | solution.py:29
  (2 other events, 4.8 us)
Sparse Core Ops, SparseCore 0:
  14.2 82.9 all-gather.2
  99.4 80.0 all-gather.4
  600.3 200.6 reduce-scatter.3
where the time goes:
time: 811 us; the launch traced here: 809 us
  waiting for transfers between devices  342 us (42%)
  starting transfers between devices  273 us (34%)
  matrix products  78.8 us (10%)
  local copies, waits for them, and re-layouts  74 us (9%)
  other arithmetic  26 us (3%)
  between operations  13.2 us (2%)
    ppermute x9, starting transfers between devices, passed_along(): return lax.ppermute(value, axis, pairs)  268 us
    unnamed x4, waiting for transfers between devices  201 us
    all_gather x1, waiting for transfers between devices, shards(): lax.all_gather(near_keys, 'patch', axis=1, tiled=True)  67.6 us
    all_gather x1, waiting for transfers between devices, shards(): lax.all_gather(near_values, 'patch', axis=1, tiled=True)  67.4 us
    unnamed x13, local copies, waits for them, and re-layouts  33.6 us
    dot_general x8, matrix products, add_block(): jnp.einsum('qhd,khd->hqk', query_heads, key_part, preferred_element_type=...  22.5 us
    squeeze x2, local copies, waits for them, and re-layouts, attend(): lax.dynamic_index_in_dim(far_values, micro_pos, 0, keepdims=False)  19.3 us
    dot_general x18, matrix products, apply_block(): jnp.dot(shifted, kernel[row_tap, col_tap], preferred_element_type=jnp.flo...  18.2 us
  transfers between devices with their start and end apart: 14, of which 5 were waited for; matrix products, arithmetic and copies ran while one was open for 4% of the time, Pallas kernels for 0%

commit v1 on v0

--- a/solution.py
+++ b/solution.py
@@ -4,6 +4,12 @@
 from jax.sharding import PartitionSpec as P
 
 HEADS = 10
+
+
+def replace_keys(inner_x):
+    return jnp.concatenate(
+        lax.all_to_all(jnp.stack(lax.axis_size("patch") * [inner_x]), "patch", 0, 0), 1
+    )
 
 
 def padded(cells, sides, width):
@@ -64,7 +70,7 @@
     near_keys = project(stale_normed, key_weight)
     near_values = project(stale_normed, value_weight)
     far_keys, far_values = (
-        lax.all_gather(near_keys, "patch", axis=1, tiled=True),
+        replace_keys(near_keys),
         lax.all_gather(near_values, "patch", axis=1, tiled=True),
     )
     far_keys = far_keys.reshape(micro_count, -1, channels)

time: 811 us -> 901 us (1.11)
  waiting for transfers between devices: 342 us -> 410 us
  local copies, waits for them, and re-layouts: 74 us -> 88.7 us
    ppermute x1, waiting for transfers between devices: 2.11 us -> 113 us  [padded(): lax.ppermute(tail, axis, [(i, (i + 1) % count) for i in range(ends)])]
    all_to_all x0 -> x1, waiting for transfers between devices: none -> 90.4 us  [replace_keys(): lax.all_to_all(jnp.stack(lax.axis_size('patch') * [inner_x]), 'patch', 0, 0)]
    all_gather x1 -> x0, waiting for transfers between devices: 67.6 us -> none  [shards(): lax.all_gather(near_keys, 'patch', axis=1, tiled=True)]
    all_gather x1, waiting for transfers between devices: 67.4 us -> 0.01 us  [shards(): lax.all_gather(near_values, 'patch', axis=1, tiled=True)]
    all_to_all x0 -> x1, local copies, waits for them, and re-layouts: none -> 9.43 us  [replace_keys(): lax.all_to_all(jnp.stack(lax.axis_size('patch') * [inner_x]), 'patch', 0, 0)]
    unnamed x4 -> x3, waiting for transfers between devices: 201 us -> 203 us
  transfers between devices with their start and end apart: 14 -> 14, of which waited for: 5 -> 4; matrix products, arithmetic and copies ran while one was open for 4% -> 5% of each run, Pallas kernels for 0% -> 0%
where the time goes in v1:
time: 901 us; the launch traced here: 899 us
  waiting for transfers between devices  410 us (46%)
  starting transfers between devices  281 us (31%)
  local copies, waits for them, and re-layouts  88.7 us (10%)
  matrix products  78 us (9%)
  other arithmetic  26 us (3%)
  between operations  13.5 us (1%)
    ppermute x9, starting transfers between devices, passed_along(): return lax.ppermute(value, axis, pairs)  268 us
    unnamed x3, waiting for transfers between devices  203 us
    ppermute x1, waiting for transfers between devices, padded(): lax.ppermute(tail, axis, [(i, (i + 1) % count) for i in range(ends)])  113 us
    all_to_all x1, waiting for transfers between devices, replace_keys(): lax.all_to_all(jnp.stack(lax.axis_size('patch') * [inner_x]), 'patch', 0, 0)  90.4 us
    unnamed x13, local copies, waits for them, and re-layouts  33.5 us
    dot_general x8, matrix products, add_block(): jnp.einsum('qhd,khd->hqk', query_heads, key_part, preferred_element_type=...  22.5 us
    squeeze x2, local copies, waits for them, and re-layouts, attend(): lax.dynamic_index_in_dim(far_values, micro_pos, 0, keepdims=False)  19.4 us
    dot_general x18, matrix products, apply_block(): jnp.dot(shifted, kernel[row_tap, col_tap], preferred_element_type=jnp.flo...  18.2 us
  transfers between devices with their start and end apart: 14, of which 4 were waited for; matrix products, arithmetic and copies ran while one was open for 5% of the time, Pallas kernels for 0%

profile of v1, /device:TPU:0, one launch (start us, length us, event | category | flops | bytes accessed | tf_op | source)
XLA Modules:
  0.0 899.1 jit_solution(3511886098156032012)
XLA Ops:
  16.0 5.4 stack.3
  21.4 8.3 all-to-all-start
  29.8 3.8 collective-permute-start.1
  34.9 113.5 %collective-permute-done.1 = bf16[2,1,64,640]{3,2,1,0:T(8,128)(2,1)S(1)} collective-permute-done((bf16[2,1,64,640]{3,2,1,0:T(8,128)(2,1)S(1)}, bf16[2,1,64,640]{3,2,1,0:T(8,128)(2,1)S(1)}, u32[]{:S(2)}, u32[]{:S(2)}) %collective-permute-start.1) | collective-permute-done | bytes 163872 | tf_op jit(solution)/shard_map/ppermute | solution.py:23
  148.4 3.2 collective-permute-done.2
  152.5 90.4 %all-to-all-done = bf16[16,2,4,64,640]{4,3,2,1,0:T(8,128)(2,1)} async-done(((bf16[16,2,4,64,640]{4,3,2,1,0:T(8,128)(2,1)}), bf16[16,2,4,64,640]{4,3,2,1,0:T(8,128)(2,1)}, u32[]{:S(2)}, u32[]{:S(2)}) %all-to-all-start) | async-done | bytes 10485792 | tf_op jit(solution)/shard_map/all_to_all | solution.py:11
  242.8 9.4 %copy.34 = bf16[16,2,4,64,640]{4,3,2,0,1:T(8,128)(2,1)} copy(bf16[16,2,4,64,640]{4,3,2,1,0:T(8,128)(2,1)} %all-to-all-done) | data formatting | bytes 20971520 | tf_op jit(solution)/shard_map/all_to_all | solution.py:11
  252.3 14.7 %copy.35 = bf16[2,4096,640]{1,2,0:T(8,128)(2,1)} copy(bf16[2,4096,640]{2,1,0:T(8,128)(2,1)} %bitcast.201) | data formatting | bytes 20971520
  267.0 14.9 %copy.36 = bf16[2,4096,640]{1,2,0:T(8,128)(2,1)} copy(bf16[2,4096,640]{2,1,0:T(8,128)(2,1)} %bitcast.216) | data formatting | bytes 20971520
  282.9 401.8 %while.41 = (s32[]{:T(128)}, f32[4,64,640]{2,1,0:T(8,128)S(1)}, bf16[2,4,64,640]{3,2,1,0:T(8,128)(2,1)}, s32[]{:T(128)}, pred[]{:T(512)}, /*index=5*/bf16[2,4,64...) while((s32[]{:T(128)}, f32[4,64,640]{2,1,0:T(8,128)S(1)}, ...), condition=%wide.region_13.14_spmd.clone, body=%wide.region_2.13_spmd.clone.sunk | while | flops 3595085824 | bytes 135619984 | solution.py:177
  283.1 58.3 %conditional.3 = (bf16[4,64,640]{2,1,0:T(8,128)(2,1)S(1)}) conditional(s32[]{:T(128)} %convert_element_type.192, () %tuple.104, (pred[]{:T(512)}, bf16[2,4,64,640]{3,2,1,0:T(8,128)(2,1)S(1)}, s32[]{:T(128)}, s32[]{:T(128)}, f32[1,640]{1,0:T(1,128)S(1)}, /*index=5*/bf16[640,640]{1,0:T(8,128)(2,1)}, bf16[640,640]{1,0:T(8,128)(2,1)}, ...), branch_computations={%region_3.3_spmd, %region_4.12_spmd.clone} | conditional | flops 3594758144 | bytes 132342232 | solution.py:165
  292.3 9.7 %dynamic-slice_bitcast_fusion = (bf16[4096,640]{0,1:T(8,128)(2,1)}, bf16[4096,640]{0,1:T(8,128)(2,1)}) fusion(bf16[2,4096,640]{1,2,0:T(8,128)(2,1)} %get-tuple-element.763, s32[]{:T(128)S(6)} %select_n.87, bf16[2,4096,640]{1,2,0:T(8,128)(2,1)} %get-tuple-element.761), kind=kLoop, calls=%fused_computation.22 | loop fusion | bytes 20971524 | tf_op jit(solution)/shard_map/while/body/eval_jaxpr/cond/branch_1_fun/jit(dynamic_index_in_dim)/squeeze | solution.py:85
  302.0 27.1 %while.40 = (s32[]{:T(128)}, f32[10,256]{1,0:T(8,128)S(1)}, f32[256,10,64]{0,2,1:T(8,128)S(1)}, bf16[4096,640]{0,1:T(8,128)(2,1)}, bf16[256,10,64]{0,2,1:T(8,128...) while((s32[]{:T(128)}, f32[10,256]{1,0:T(8,128)S(1)}, ...), condition=%wide.region_10.9_spmd, body=%wide.region_8.8_spmd.sunk | while | flops 686999552 | bytes 30527656 | solution.py:129
  344.6 58.3 %conditional.3 = (bf16[4,64,640]{2,1,0:T(8,128)(2,1)S(1)}) conditional(s32[]{:T(128)} %convert_element_type.192, () %tuple.104, (pred[]{:T(512)}, bf16[2,4,64,640]{3,2,1,0:T(8,128)(2,1)S(1)}, s32[]{:T(128)}, s32[]{:T(128)}, f32[1,640]{1,0:T(1,128)S(1)}, /*index=5*/bf16[640,640]{1,0:T(8,128)(2,1)}, bf16[640,640]{1,0:T(8,128)(2,1)}, ...), branch_computations={%region_3.3_spmd, %region_4.12_spmd.clone} | conditional | flops 3594758144 | bytes 132342232 | solution.py:165
  353.8 9.7 %dynamic-slice_bitcast_fusion = (bf16[4096,640]{0,1:T(8,128)(2,1)}, bf16[4096,640]{0,1:T(8,128)(2,1)}) fusion(bf16[2,4096,640]{1,2,0:T(8,128)(2,1)} %get-tuple-element.763, s32[]{:T(128)S(6)} %select_n.87, bf16[2,4096,640]{1,2,0:T(8,128)(2,1)} %get-tuple-element.761), kind=kLoop, calls=%fused_computation.22 | loop fusion | bytes 20971524 | tf_op jit(solution)/shard_map/while/body/eval_jaxpr/cond/branch_1_fun/jit(dynamic_index_in_dim)/squeeze | solution.py:85
  363.5 27.1 %while.40 = (s32[]{:T(128)}, f32[10,256]{1,0:T(8,128)S(1)}, f32[256,10,64]{0,2,1:T(8,128)S(1)}, bf16[4096,640]{0,1:T(8,128)(2,1)}, bf16[256,10,64]{0,2,1:T(8,128...) while((s32[]{:T(128)}, f32[10,256]{1,0:T(8,128)S(1)}, ...), condition=%wide.region_10.9_spmd, body=%wide.region_8.8_spmd.sunk | while | flops 686999552 | bytes 30527656 | solution.py:129
  406.5 62.4 %collective-permute-start = (bf16[4,64,640]{2,1,0:T(8,128)(2,1)S(1)}, bf16[4,64,640]{2,1,0:T(8,128)(2,1)S(1)}, u32[]{:S(2)}, u32[]{:S(2)}) collective-permute-start(bf16[4,64,640]{2,1,0:T(8,128)(2,1)S(1)} %get-tuple-element.1118), channel_id=1, source_target_pairs={{0,16},{16,32},{32,48},{48,64},{64,80},{80,96},{96,112},{1,17},{17... | collective-permute-start | bytes 983048 | tf_op jit(solution)/shard_map/while/body/eval_jaxpr/ppermute | solution.py:35
  470.8 6.6 collective-permute-start
  479.4 64.8 %collective-permute-start = (bf16[4,64,640]{2,1,0:T(8,128)(2,1)S(1)}, bf16[4,64,640]{2,1,0:T(8,128)(2,1)S(1)}, u32[]{:S(2)}, u32[]{:S(2)}) collective-permute-start(bf16[4,64,640]{2,1,0:T(8,128)(2,1)S(1)} %get-tuple-element.1118), channel_id=1, source_target_pairs={{0,16},{16,32},{32,48},{48,64},{64,80},{80,96},{96,112},{1,17},{17... | collective-permute-start | bytes 983048 | tf_op jit(solution)/shard_map/while/body/eval_jaxpr/ppermute | solution.py:35
  546.1 6.6 collective-permute-start
  554.7 55.3 %collective-permute-start = (bf16[4,64,640]{2,1,0:T(8,128)(2,1)S(1)}, bf16[4,64,640]{2,1,0:T(8,128)(2,1)S(1)}, u32[]{:S(2)}, u32[]{:S(2)}) collective-permute-start(bf16[4,64,640]{2,1,0:T(8,128)(2,1)S(1)} %get-tuple-element.1118), channel_id=1, source_target_pairs={{0,16},{16,32},{32,48},{48,64},{64,80},{80,96},{96,112},{1,17},{17... | collective-permute-start | bytes 983048 | tf_op jit(solution)/shard_map/while/body/eval_jaxpr/ppermute | solution.py:35
  611.9 6.6 collective-permute-start
  620.5 62.4 %collective-permute-start = (bf16[4,64,640]{2,1,0:T(8,128)(2,1)S(1)}, bf16[4,64,640]{2,1,0:T(8,128)(2,1)S(1)}, u32[]{:S(2)}, u32[]{:S(2)}) collective-permute-start(bf16[4,64,640]{2,1,0:T(8,128)(2,1)S(1)} %get-tuple-element.1118), channel_id=1, source_target_pairs={{0,16},{16,32},{32,48},{48,64},{64,80},{80,96},{96,112},{1,17},{17... | collective-permute-start | bytes 983048 | tf_op jit(solution)/shard_map/while/body/eval_jaxpr/ppermute | solution.py:35
  687.6 203.0 %reduce-scatter.4.cloned.1.call-done = bf16[8,5120]{1,0:T(8,128)(2,1)} async-done(((bf16[64,5120]{1,0:T(8,128)(2,1)}), bf16[8,5120]{1,0:T(8,128)(2,1)}) %reduce-scatter.4.cloned.1.call-update) | async-done | bytes 81936
  (203 shorter events, 133.6 us)
Async XLA Ops:
  6.5 260.5 %all-gather.2.cloned.1.call-start = ((), (), s32[]{:S(2)}) async-start(), calls=%async_computation.2 | async-start | bytes 11141120 | tf_op jit(solution)/shard_map/all_gather | solution.py:74
  21.4 8.4 copy-start.3
  21.4 221.5 %all-to-all-start = ((bf16[16,2,4,64,640]{4,3,2,1,0:T(8,128)(2,1)}), bf16[16,2,4,64,640]{4,3,2,1,0:T(8,128)(2,1)}, u32[]{:S(2)}, u32[]{:S(2)}) async-start(bf16[16,2,4,64,640]{4,3,2,1,0:T(8,128)(2,1)} %stack.3), calls=%async_computation | async-start | bytes 20971520 | tf_op jit(solution)/shard_map/all_to_all | solution.py:11
  29.7 860.9 %reduce-scatter.4.cloned.1.call-start = ((), (), s32[]{:S(2)}) async-start(), calls=%async_computation.3 | async-start | bytes 737280
  29.8 118.6 %collective-permute-start.1 = (bf16[2,1,64,640]{3,2,1,0:T(8,128)(2,1)S(1)}, bf16[2,1,64,640]{3,2,1,0:T(8,128)(2,1)S(1)}, u32[]{:S(2)}, u32[]{:S(2)}) collective-permute-start(bf16[2,1,64,640]{3,2,1,0:T(8,128)(2,1)S(1)} %get-tuple-element.860), channel_id=1, source_target_pairs={{0,1},{1,2},{2,3},{3,4},{4,5},{5,6},{6,7},{7,8},{8,9},{9,10},{10,1... | collective-permute-start | bytes 491528 | tf_op jit(solution)/shard_map/ppermute | solution.py:23
  33.6 118.0 %collective-permute-start.2 = (bf16[2,1,64,640]{3,2,1,0:T(8,128)(2,1)S(1)}, bf16[2,1,64,640]{3,2,1,0:T(8,128)(2,1)S(1)}, u32[]{:S(2)}, u32[]{:S(2)}) collective-permute-start(bf16[2,1,64,640]{3,2,1,0:T(8,128)(2,1)S(1)} %get-tuple-element.861), channel_id=1, source_target_pairs={{1,0},{2,1},{3,2},{4,3},{5,4},{6,5},{7,6},{8,7},{9,8},{10,9},{11,1... | collective-permute-start | bytes 491528 | tf_op jit(solution)/shard_map/ppermute | solution.py:25
  267.0 15.8 %copy-start = (bf16[2,4,64,640]{3,2,1,0:T(8,128)(2,1)S(1)}, bf16[2,4,64,640]{3,2,1,0:T(8,128)(2,1)}, u32[]{:S(2)}) copy-start(bf16[2,4,64,640]{3,2,1,0:T(8,128)(2,1)} %param.16) | copy-start | bytes 1966084
  267.0 15.8 %copy-start.4 = (f32[1,640]{1,0:T(1,128)S(1)}, f32[1,640]{1,0:T(1,128)}, u32[]{:S(2)}) copy-start(f32[1,640]{1,0:T(1,128)} %param.19) | copy-start | bytes 7684
  267.0 15.8 %copy-start.5 = (f32[1,640]{1,0:T(1,128)S(1)}, f32[1,640]{1,0:T(1,128)}, u32[]{:S(2)}) copy-start(f32[1,640]{1,0:T(1,128)} %param.24) | copy-start | bytes 7684
  283.1 6.3 copy-start.2
  302.0 27.5 %copy-start.1 = (bf16[640,640]{1,0:T(8,128)(2,1)S(1)}, bf16[640,640]{1,0:T(8,128)(2,1)}, u32[]{:S(2)}) copy-start(bf16[640,640]{1,0:T(8,128)(2,1)} %get-tuple-element.766) | copy-start | bytes 2457604 | tf_op jit(solution)/shard_map/while/body/eval_jaxpr/cond
  331.6 7.3 slice-start
  341.4 3.1 collective-permute-start
  344.6 6.3 copy-start.2
  363.5 27.5 %copy-start.1 = (bf16[640,640]{1,0:T(8,128)(2,1)S(1)}, bf16[640,640]{1,0:T(8,128)(2,1)}, u32[]{:S(2)}) copy-start(bf16[640,640]{1,0:T(8,128)(2,1)} %get-tuple-element.766) | copy-start | bytes 2457604 | tf_op jit(solution)/shard_map/while/body/eval_jaxpr/cond
  393.1 7.3 slice-start
  402.9 3.5 collective-permute-start
  406.5 64.2 %collective-permute-start = (bf16[4,64,640]{2,1,0:T(8,128)(2,1)S(1)}, bf16[4,64,640]{2,1,0:T(8,128)(2,1)S(1)}, u32[]{:S(2)}, u32[]{:S(2)}) collective-permute-start(bf16[4,64,640]{2,1,0:T(8,128)(2,1)S(1)} %get-tuple-element.1118), channel_id=1, source_target_pairs={{0,16},{16,32},{32,48},{48,64},{64,80},{80,96},{96,112},{1,17},{17... | collective-permute-start | bytes 983048 | tf_op jit(solution)/shard_map/while/body/eval_jaxpr/ppermute | solution.py:35
  470.8 8.4 collective-permute-start
  479.4 66.6 %collective-permute-start = (bf16[4,64,640]{2,1,0:T(8,128)(2,1)S(1)}, bf16[4,64,640]{2,1,0:T(8,128)(2,1)S(1)}, u32[]{:S(2)}, u32[]{:S(2)}) collective-permute-start(bf16[4,64,640]{2,1,0:T(8,128)(2,1)S(1)} %get-tuple-element.1118), channel_id=1, source_target_pairs={{0,16},{16,32},{32,48},{48,64},{64,80},{80,96},{96,112},{1,17},{17... | collective-permute-start | bytes 983048 | tf_op jit(solution)/shard_map/while/body/eval_jaxpr/ppermute | solution.py:35
  546.1 8.4 collective-permute-start
  554.7 57.1 %collective-permute-start = (bf16[4,64,640]{2,1,0:T(8,128)(2,1)S(1)}, bf16[4,64,640]{2,1,0:T(8,128)(2,1)S(1)}, u32[]{:S(2)}, u32[]{:S(2)}) collective-permute-start(bf16[4,64,640]{2,1,0:T(8,128)(2,1)S(1)} %get-tuple-element.1118), channel_id=1, source_target_pairs={{0,16},{16,32},{32,48},{48,64},{64,80},{80,96},{96,112},{1,17},{17... | collective-permute-start | bytes 983048 | tf_op jit(solution)/shard_map/while/body/eval_jaxpr/ppermute | solution.py:35
  611.9 8.4 collective-permute-start
  620.5 64.2 %collective-permute-start = (bf16[4,64,640]{2,1,0:T(8,128)(2,1)S(1)}, bf16[4,64,640]{2,1,0:T(8,128)(2,1)S(1)}, u32[]{:S(2)}, u32[]{:S(2)}) collective-permute-start(bf16[4,64,640]{2,1,0:T(8,128)(2,1)S(1)} %get-tuple-element.1118), channel_id=1, source_target_pairs={{0,16},{16,32},{32,48},{48,64},{64,80},{80,96},{96,112},{1,17},{17... | collective-permute-start | bytes 983048 | tf_op jit(solution)/shard_map/while/body/eval_jaxpr/ppermute | solution.py:35
  (2 other events, 10.2 us)
Sparse Core Ops, SparseCore 0:
  14.2 230.7 all-gather.1
  687.8 202.8 reduce-scatter.3
